TPU v7x, 512 devices: a whole 4x8x8 slice. The times are simulated.
512 devices in a mesh: sector: 64 (over x, z, core), mpo: 8 (over y).
Axes of the slice: x: 4, y: 8, z: 8, core: 2. Of those that a mesh axis runs over, the one named last changes fastest.
Arguments:
- wavefunction: bfloat16 [64, 512, 512], P('sector'), may hold values from -6 to 6
- env_left: bfloat16 [32, 64, 512, 512], P('mpo', 'sector'), may hold values from -0.25 to 0.25
- env_right: bfloat16 [32, 64, 512, 512], P('mpo', 'sector'), may hold values from -0.046875 to 0.046875
- row_len: int32 [64], P('sector'), may hold values from 1 to 512, 20480 in all
- col_len: int32 [64], P('sector'), may hold values from 1 to 512, 20480 in all
- charge_shift: int32 [32], P('mpo'), may hold values from -1 to 1
- present: int32 [32, 64], P('mpo', 'sector'), may hold values 0 or 1
Outputs:
- first_image: bfloat16 [64, 512, 512], P('sector', 'mpo')
- second_image: bfloat16 [64, 512, 512], P('sector', 'mpo')
All inputs are finite; a program needn't handle non-finite values. No bound on the sum of `row_len` or of `col_len` or of `present` on one device may be relied on, other than what follows from the above.
Results may differ from a plain program's by a relative error of at most 0.0065.
Values may be sent and summed in bfloat16 or wider, within the bound.
A program may use at most 64 MiB of HBM per device.

v0:
```python
import jax
import jax.numpy as jnp
from jax import lax
from jax.sharding import PartitionSpec as P

epsilon = 1e-06


def with_halo(cells, sides, width):
    for axis, dim in sides:
        count = lax.axis_size(axis)
        ends = count - 1
        head = lax.slice_in_dim(cells, 0, width, axis=dim)
        tail = lax.slice_in_dim(cells, cells.shape[dim] - width, cells.shape[dim], axis=dim)
        cells = jnp.concatenate(
            [
                lax.ppermute(tail, axis, [(i, (i + 1) % count) for i in range(ends)]),
                cells,
                lax.ppermute(head, axis, [((i + 1) % count, i) for i in range(ends)]),
            ],
            axis=dim,
        )
    return cells


def image_rows(padded, left_envs, right_envs, shifts, weights):
    upper = shifts[:, None, None]
    selected = jnp.where(
        upper == 1, padded[0][None], jnp.where(upper == 0, padded[1][None], padded[2][None])
    )
    inner_part = jnp.einsum("wij,wjk->wik", left_envs, selected, preferred_element_type=jnp.float32)
    inner_part = (inner_part * weights[:, None, None]).astype(jnp.bfloat16)
    return jnp.einsum("wij,wkj->ik", inner_part, right_envs, preferred_element_type=jnp.float32)


def neighbours(source_field):
    return with_halo(source_field[None], (("sector", 0),), 1)


def shards(wavefunction, env_left, env_right, row_len, col_len, charge_shift, present):
    block_width = wavefunction.shape[1]
    mpo_parts = lax.axis_size("mpo")
    sectors = lax.axis_size("sector")
    share_rows = block_width // mpo_parts
    position = jnp.arange(block_width, dtype=jnp.int32)
    row_mask = (position < row_len[0]).astype(jnp.float32)
    col_mask = (position < col_len[0]).astype(jnp.float32)
    cell_mask = row_mask[:, None] * col_mask[None, :]
    first_field = (wavefunction[0] * cell_mask).astype(jnp.bfloat16)
    left_envs = env_left[:, 0]
    right_envs = env_right[:, 0]
    weights = present[:, 0].astype(jnp.float32)
    offset = lax.axis_index("mpo") * share_rows
    cell_count = sectors * block_width * block_width

    def full_image(source_field):
        padded = neighbours(source_field)
        partial_sum = image_rows(padded, left_envs, right_envs, charge_shift, weights)
        return lax.psum(partial_sum, "mpo") * cell_mask

    first_full = full_image(first_field)
    norm_sum = lax.psum(jnp.sum(first_full * first_full), "sector")
    basis_vector = (first_full * (1.0 / jnp.sqrt(norm_sum / cell_count + epsilon))).astype(
        jnp.bfloat16
    )
    second_full = full_image(basis_vector)
    first_share = lax.dynamic_slice_in_dim(first_full, offset, share_rows, 0)
    second_share = lax.dynamic_slice_in_dim(second_full, offset, share_rows, 0)
    return (first_share.astype(jnp.bfloat16)[None], second_share.astype(jnp.bfloat16)[None])


def solution(mesh):
    in_specs = (
        P("sector", None, None),
        P("mpo", "sector", None, None),
        P("mpo", "sector", None, None),
        P("sector"),
        P("sector"),
        P("mpo"),
        P("mpo", "sector"),
    )
    out_specs = (P("sector", "mpo", None), P("sector", "mpo", None))
    return jax.shard_map(shards, mesh=mesh, in_specs=in_specs, out_specs=out_specs, check_vma=False)
```

profile of v0, /device:TPU:6, one launch (start us, length us, event | category | flops | bytes accessed | tf_op | source)
XLA Modules:
  0.0 346.5 jit_solution(3624171714998462297)
XLA Ops:
  7.2 0.0 copy-start
  7.2 0.0 all-reduce.3.cloned.1.call-start
  8.7 1.2 multiply_convert_fusion.3
  9.9 10.7 %collective-permute-start.1 = (bf16[1,512,512]{2,1,0:T(8,128)(2,1)S(1)}, bf16[1,512,512]{2,1,0:T(8,128)(2,1)S(1)}, u32[]{:S(2)}, u32[]{:S(2)}) collective-permute-start(bf16[1,512,512]{2,1,0:T(8,128)(2,1)S(1)} %multiply_convert_fusion.3), channel_id=1, source_target_pairs={{8,0},{16,8},{24,16},{32,24},{40,32},{48,40},{56,48},{64,56},{72,6... | collective-permute-start | bytes 1572872 | tf_op jit(solution)/shard_map/ppermute | solution.py:19
  20.6 1.9 collective-permute-start
  22.5 0.7 convert_bitcast_fusion
  23.2 0.7 broadcast_compare_fusion.1
  23.8 1.2 fusion.62
  25.0 2.2 collective-permute-done.1
  27.2 5.9 %collective-permute-done = bf16[1,512,512]{2,1,0:T(8,128)(2,1)S(1)} collective-permute-done((bf16[1,512,512]{2,1,0:T(8,128)(2,1)S(1)}, bf16[1,512,512]{2,1,0:T(8,128)(2,1)S(1)}, u32[]{:S(2)}, u32[]{:S(2)}) %collective-permute-start) | collective-permute-done | bytes 524320 | tf_op jit(solution)/shard_map/ppermute | solution.py:17
  33.2 0.0 copy-start.2
  33.2 0.8 copy-done.2
  34.0 0.0 copy-done
  34.0 5.3 %fusion.16 = f32[512,512]{1,0:T(8,128)} fusion(bf16[4,1,512,512]{3,2,1,0:T(8,128)(2,1)S(1)} %copy-done, bf16[4,1,512,512]{3,2,1,0:T(8,128)(2,1)} %param.8, f32[4]{0:T(128)S(1)} %convert_bitcast_fusion, pred[4]{0:T(512)(128)(4,1)S(1)} %get-tuple-element.6, pred[4]{0:T(512)(128)(4,1)S(1)} %get-tuple-element.5, bf16[512,512]{1,0:T(8,128)(2,1)S(1)} %bitcast.54, ...), kind=kOutput, calls=%fused_computation.18 | convolution fusion | flops 2151677952 | bytes 6815768 | tf_op jit(solution)/shard_map/wij,wkj->ik/dot_general | solution.py:33
  39.3 0.0 all-reduce.3.cloned.1.call-update
  39.4 0.0 all-reduce.5.cloned.1.call-start
  39.4 77.1 %all-reduce.3.cloned.1.call-done = f32[512,512]{1,0:T(8,128)} async-done(((f32[512,512]{1,0:T(8,128)}), f32[512,512]{1,0:T(8,128)}) %all-reduce.3.cloned.1.call-update) | async-done | bytes 1048592 | tf_op jit(solution)/shard_map/psum | solution.py:59
  116.5 3.0 multiply_reduce_fusion
  119.5 105.3 %psum.22 = f32[]{:T(128)} all-reduce(f32[]{:T(128)} %get-tuple-element.2), channel_id=1, replica_groups=mesh['sector'=64,'mpo'=8] {'sector'}, use_global_device_ids=true, to_apply=%region_2.3 | all-reduce | flops 1 | bytes 8 | tf_op jit(solution)/shard_map/psum | solution.py:62
  225.5 0.1 fusion.61
  225.6 1.9 collective-permute-start.3
  227.6 2.4 collective-permute-start.2
  230.0 0.9 multiply_convert_fusion.2
  230.9 3.3 collective-permute-done.3
  234.2 5.9 %collective-permute-done.2 = bf16[1,512,512]{2,1,0:T(8,128)(2,1)S(1)} collective-permute-done((bf16[1,512,512]{2,1,0:T(8,128)(2,1)S(1)}, bf16[1,512,512]{2,1,0:T(8,128)(2,1)S(1)}, u32[]{:S(2)}, u32[]{:S(2)}) %collective-permute-start.2) | collective-permute-done | bytes 524320 | tf_op jit(solution)/shard_map/ppermute | solution.py:17
  240.2 0.0 copy-done.1
  240.2 0.8 copy-done.3
  241.0 5.7 %fusion.21 = f32[512,512]{1,0:T(8,128)} fusion(bf16[4,1,512,512]{3,2,1,0:T(8,128)(2,1)S(1)} %copy-done, bf16[4,1,512,512]{3,2,1,0:T(8,128)(2,1)} %param.8, f32[4]{0:T(128)S(1)} %convert_bitcast_fusion, pred[4]{0:T(512)(128)(4,1)S(1)} %get-tuple-element.6, pred[4]{0:T(512)(128)(4,1)S(1)} %get-tuple-element.5, bf16[512,512]{1,0:T(8,128)(2,1)} %bitcast.55, ...), kind=kOutput, calls=%fused_computation.19 | convolution fusion | flops 2151677952 | bytes 6815768 | tf_op jit(solution)/shard_map/wij,wkj->ik/dot_general | solution.py:33
  246.7 0.0 all-reduce.5.cloned.1.call-update
  246.7 0.6 fusion.56
  247.3 90.7 %all-reduce.5.cloned.1.call-done = f32[512,512]{1,0:T(8,128)} async-done(((f32[512,512]{1,0:T(8,128)}), f32[512,512]{1,0:T(8,128)}) %all-reduce.5.cloned.1.call-update) | async-done | bytes 1048592 | tf_op jit(solution)/shard_map/psum | solution.py:59
  338.1 1.6 fusion.57
  (3 shorter events, 0.0 us)
Async XLA Ops:
  7.2 26.8 %copy-start = (bf16[4,1,512,512]{3,2,1,0:T(8,128)(2,1)S(1)}, bf16[4,1,512,512]{3,2,1,0:T(8,128)(2,1)}, u32[]{:S(2)}) copy-start(bf16[4,1,512,512]{3,2,1,0:T(8,128)(2,1)} %param.9) | copy-start | bytes 6291460
  7.2 109.3 %all-reduce.3.cloned.1.call-start = ((), (), s32[]{:S(2)}) async-start(), calls=%async_computation | async-start | bytes 2097152 | tf_op jit(solution)/shard_map/psum | solution.py:59
  9.9 17.3 %collective-permute-start.1 = (bf16[1,512,512]{2,1,0:T(8,128)(2,1)S(1)}, bf16[1,512,512]{2,1,0:T(8,128)(2,1)S(1)}, u32[]{:S(2)}, u32[]{:S(2)}) collective-permute-start(bf16[1,512,512]{2,1,0:T(8,128)(2,1)S(1)} %multiply_convert_fusion.3), channel_id=1, source_target_pairs={{8,0},{16,8},{24,16},{32,24},{40,32},{48,40},{56,48},{64,56},{72,6... | collective-permute-start | bytes 1572872 | tf_op jit(solution)/shard_map/ppermute | solution.py:19
  20.6 12.6 %collective-permute-start = (bf16[1,512,512]{2,1,0:T(8,128)(2,1)S(1)}, bf16[1,512,512]{2,1,0:T(8,128)(2,1)S(1)}, u32[]{:S(2)}, u32[]{:S(2)}) collective-permute-start(bf16[1,512,512]{2,1,0:T(8,128)(2,1)S(1)} %multiply_convert_fusion.3), channel_id=1, source_target_pairs={{0,8},{8,16},{16,24},{24,32},{32,40},{40,48},{48,56},{56,64},{64,7... | collective-permute-start | bytes 1572872 | tf_op jit(solution)/shard_map/ppermute | solution.py:17
  33.2 0.8 copy-start.2
  39.4 298.7 %all-reduce.5.cloned.1.call-start = ((), (), s32[]{:S(2)}) async-start(), calls=%async_computation.1 | async-start | bytes 2097152 | tf_op jit(solution)/shard_map/psum | solution.py:59
  225.6 8.6 %collective-permute-start.3 = (bf16[1,512,512]{2,1,0:T(8,128)(2,1)S(1)}, bf16[1,512,512]{2,1,0:T(8,128)(2,1)S(1)}, u32[]{:S(2)}, u32[]{:S(2)}) collective-permute-start(bf16[1,512,512]{2,1,0:T(8,128)(2,1)S(1)} %fusion.61), channel_id=1, source_target_pairs={{8,0},{16,8},{24,16},{32,24},{40,32},{48,40},{56,48},{64,56},{72,6... | collective-permute-start | bytes 1572872 | tf_op jit(solution)/shard_map/ppermute | solution.py:19
  227.6 12.6 %collective-permute-start.2 = (bf16[1,512,512]{2,1,0:T(8,128)(2,1)S(1)}, bf16[1,512,512]{2,1,0:T(8,128)(2,1)S(1)}, u32[]{:S(2)}, u32[]{:S(2)}) collective-permute-start(bf16[1,512,512]{2,1,0:T(8,128)(2,1)S(1)} %fusion.61), channel_id=1, source_target_pairs={{0,8},{8,16},{16,24},{24,32},{32,40},{40,48},{48,56},{56,64},{64,7... | collective-permute-start | bytes 1572872 | tf_op jit(solution)/shard_map/ppermute | solution.py:17
  234.2 5.9 %copy-start.1 = (bf16[1,512,512]{2,1,0:T(8,128)(2,1)}, bf16[1,512,512]{2,1,0:T(8,128)(2,1)S(1)}, u32[]{:S(2)}) copy-start(bf16[1,512,512]{2,1,0:T(8,128)(2,1)S(1)} %collective-permute-done.3) | copy-start | bytes 1572868
  240.2 0.8 copy-start.3
Sparse Core Ops, SparseCore 0:
  39.5 76.9 all-reduce.2
  246.8 91.2 all-reduce.4
where the time goes:
time: 347 us
  waiting for transfers between devices  185 us (53%)
  blocking collectives  105 us (30%)
  starting transfers between devices  17 us (5%)
  between operations  16.2 us (5%)
  matrix products  11.1 us (3%)
  other arithmetic  9.43 us (3%)
    psum x2, waiting for transfers between devices, full_image(): return lax.psum(partial_sum, 'mpo') * cell_mask  168 us
    psum x1, blocking collectives, shards(): norm_sum = lax.psum(jnp.sum(first_full * first_full), 'sector')  105 us
    ppermute x2, starting transfers between devices, with_halo(): lax.ppermute(head, axis, [((i + 1) % count, i) for i in range(ends)])  12.6 us
    ppermute x2, waiting for transfers between devices, with_halo(): lax.ppermute(tail, axis, [(i, (i + 1) % count) for i in range(ends)])  11.9 us
    dot_general x2, matrix products, image_rows(): jnp.einsum('wij,wkj->ik', inner_part, right_envs, preferred_element_type=...  11.1 us
  transfers between devices with their start and end apart: 6, of which 6 were waited for; matrix products, arithmetic and copies ran while one was open for 1% of the time, Pallas kernels for 0%

commit v1 on v0

v1 whole, which is shorter than its diff:
```python
import functools

import jax
import jax.numpy as jnp
from jax import lax
from jax.experimental import pallas as pl
from jax.experimental.pallas import tpu as pltpu
from jax.sharding import PartitionSpec as P

epsilon = 1e-06
MESH = pl.DeviceIdType.MESH
F32, BF16 = jnp.float32, jnp.bfloat16
CHUNKS = 4


def kernel(dims, wave, env_left, env_right, row_len, col_len, shift, present, out1, out2,
           raw, rmat, rtrans, lcat, u, own, rs_send, rs_recv, sq_send, sq_y, sq_z, sq_x, sq_c, obuf,
           ld, ss, rs, *fields):
    n, ns, nx, nz, wl, b = dims
    h = n // 2
    share = b // n
    crow = b // CHUNKS
    v1, v2 = fields[:CHUNKS], fields[CHUNKS:]

    s = lax.axis_index("sector")
    y = lax.axis_index("mpo")
    core = lax.rem(s, 2)
    z = lax.rem(s // 2, nz)
    x = s // (2 * nz)
    near_s = s + 1 - 2 * core
    far_s = lax.rem(s + ns + 2 * core - 1, ns)
    near, far = (near_s, y), (far_s, y)

    def ypeer(k):
        return (s, lax.rem(y + n + k, n))

    def zpeer(k):
        return ((x * nz + lax.rem(z + k, nz)) * 2 + core, y)

    def xpeer(k):
        return ((lax.rem(x + k, nx) * nz + z) * 2 + core, y)

    bar = pltpu.get_barrier_semaphore()
    partners = [ypeer(k) for k in range(1, n)] + [near, far]
    partners += [zpeer(k) for k in range(1, nz)] + [xpeer(k) for k in range(1, nx)]
    for p in partners:
        pl.semaphore_signal(bar, inc=1, device_id=p, device_id_type=MESH)

    load_wave = pltpu.make_async_copy(wave.at[0], raw, ld.at[0])
    load_wave.start()
    load_r, load_l = [], []
    for w in range(wl):
        c = pltpu.make_async_copy(env_right.at[w, 0], rmat.at[w], ld.at[1 + w])
        c.start()
        load_r.append(c)
    for w in range(wl):
        c = pltpu.make_async_copy(env_left.at[w, 0], lcat.at[:, w * b:(w + 1) * b], ld.at[1 + wl + w])
        c.start()
        load_l.append(c)

    rl, cl = row_len[0], col_len[0]
    near_shift = 2 * core - 1
    slot, weight = [], []
    for w in range(wl):
        sh = shift[w]
        source = s - sh
        slot.append(jnp.where(sh == 0, 0, jnp.where(sh == near_shift, 1, 2)))
        ok = jnp.logical_and(source >= 0, source < ns)
        weight.append(jnp.where(ok, present[w, 0], 0).astype(F32))

    sends = []
    counter = [0]
    sem_of = {}

    def sem(key):
        if key not in sem_of:
            sem_of[key] = counter[0]
            counter[0] += 1
        return sem_of[key]

    def send(src, dst, key, dev):
        i = sem(key)
        c = pltpu.make_async_remote_copy(src, dst, ss.at[i], rs.at[i], device_id=dev, device_id_type=MESH)
        c.start()
        sends.append(c)

    def arrived(dst, key):
        i = sem(key)
        pltpu.make_async_remote_copy(dst, dst, ss.at[i], rs.at[i], device_id=near, device_id_type=MESH).wait_recv()

    load_wave.wait()
    cmask = lax.broadcasted_iota(jnp.int32, (crow, b), 1) < cl
    rio = lax.broadcasted_iota(jnp.int32, (crow, b), 0)
    for c in range(CHUNKS):
        keep = jnp.logical_and(cmask, rio + c * crow < rl)
        v1[c][0] = jnp.where(keep, raw[c * crow:(c + 1) * crow, :].astype(F32), 0.0).astype(BF16)
    pl.semaphore_wait(bar, len(partners))
    for c in range(CHUNKS):
        send(v1[c].at[0], v1[c].at[2], ("h1f", c), far)
        send(v1[c].at[0], v1[c].at[1], ("h1n", c), near)

    for w in range(wl):
        load_r[w].wait()
        rtrans[w] = rmat[w].T
    for w in range(wl):
        load_l[w].wait()

    for c in range(CHUNKS):
        arrived(v1[c].at[1], ("h1n", c))
        arrived(v1[c].at[2], ("h1f", c))
        for w in range(wl):
            part = jnp.dot(v1[c][slot[w]], rtrans[w], preferred_element_type=F32)
            u[w * b + c * crow:w * b + (c + 1) * crow, :] = (part * weight[w]).astype(BF16)

    def start(k):
        return pl.multiple_of(lax.rem(y + n + k, n) * share, share)

    order = [h]
    for k in range(h - 1, 0, -1):
        order += [k, -k]
    order += [0]

    def reduce_scatter(app, between):
        for a in range(0, n, 2):
            k0, k1 = order[a], order[a + 1]
            lhs = jnp.concatenate([lcat[pl.ds(start(k0), share), :], lcat[pl.ds(start(k1), share), :]], axis=0)
            part = jnp.dot(lhs, u[...], preferred_element_type=F32)
            for k, block in ((k0, part[:share]), (k1, part[share:])):
                if k == 0:
                    own[...] = block
                else:
                    rs_send[app, k % n] = block.astype(BF16)
                    send(rs_send.at[app, k % n], rs_recv.at[app, k % n], ("rs", app, k), ypeer(k))
        between()
        total = own[...]
        for k in order[:-1]:
            arrived(rs_recv.at[app, k % n], ("rs", app, k))
            total = total + rs_recv[app, k % n].astype(F32)
        keep_r = lax.broadcasted_iota(jnp.int32, (share, b), 0) + y * share < rl
        keep_c = lax.broadcasted_iota(jnp.int32, (share, b), 1) < cl
        return jnp.where(jnp.logical_and(keep_r, keep_c), total, 0.0)

    image = reduce_scatter(0, lambda: None)

    def field(r, layer):
        if r in (0, h):
            return v2[0].at[layer, 0 if r == 0 else 1]
        return v2[abs(r)].at[layer, 0 if r > 0 else 1]

    v2[0][0, 0] = image.astype(BF16)
    square = image * image
    square = jnp.sum(square.reshape(share // 8, 8, b), axis=0)
    tile = square[:, 0:128]
    for q in range(128, b, 128):
        tile = tile + square[:, q:q + 128]
    sq_send[0] = tile

    def hand_on(r):
        send(field(r, 0), field(r, 2), ("h2f", r), far)
        send(field(r, 0), field(r, 1), ("h2n", r), near)

    near_first = []
    for k in range(1, h):
        near_first += [k, -k]
    near_first += [h]
    for k in near_first:
        send(field(0, 0), field(h if k == h else -k, 0), ("ag", h if k == h else -k), ypeer(k))
    hand_on(0)
    for k in range(1, n):
        send(sq_send.at[0], sq_y.at[k - 1], ("sqy", k), ypeer(k))
    write1 = pltpu.make_async_copy(v2[0].at[0, 0], out1.at[0], ld.at[0])
    write1.start()

    for r in near_first:
        arrived(field(r, 0), ("ag", r))
        hand_on(r)

    total = sq_send[0]
    for k in range(1, n):
        arrived(sq_y.at[k - 1], ("sqy", k))
        total = total + sq_y[k - 1]
    sq_send[1] = total
    for k in range(1, nz):
        send(sq_send.at[1], sq_z.at[k - 1], ("sqz", k), zpeer(k))

    for g in list(range(1, h)) + [0]:
        members = (g, -g) if g else (0, h)
        for r in members:
            arrived(field(r, 1), ("h2n", r))
            arrived(field(r, 2), ("h2f", r))
        for w in range(wl):
            lhs = v2[g][slot[w]].reshape(2 * share, b)
            part = (jnp.dot(lhs, rtrans[w], preferred_element_type=F32) * weight[w]).astype(BF16)
            for i, r in enumerate(members):
                u[pl.ds(w * b + start(r), share), :] = part[i * share:(i + 1) * share]

    def norm_steps():
        total = sq_send[1]
        for k in range(1, nz):
            arrived(sq_z.at[k - 1], ("sqz", k))
            total = total + sq_z[k - 1]
        sq_send[2] = total
        for k in range(1, nx):
            send(sq_send.at[2], sq_x.at[k - 1], ("sqx", k), xpeer(k))
        for k in range(1, nx):
            arrived(sq_x.at[k - 1], ("sqx", k))
            total = total + sq_x[k - 1]
        sq_send[3] = total
        send(sq_send.at[3], sq_c, ("sqc", 0), near)
        arrived(sq_c, ("sqc", 0))
        sq_send[4] = total + sq_c[...]

    second = reduce_scatter(1, norm_steps)
    norm = jnp.sum(sq_send[4]) / (ns * b * b) + epsilon
    obuf[...] = (second * (1.0 / jnp.sqrt(jnp.full((1, 1), norm, F32)))).astype(BF16)
    write2 = pltpu.make_async_copy(obuf, out2.at[0], ld.at[1])
    write2.start()
    for c in sends:
        c.wait_send()
    write1.wait()
    write2.wait()
    assert counter[0] <= ss.shape[0]


def shards(dims, wavefunction, env_left, env_right, row_len, col_len, charge_shift, present):
    n, ns, nx, nz, wl, b = dims
    share, crow = b // n, b // CHUNKS
    any_spec = pl.BlockSpec(memory_space=pl.ANY)
    smem = pl.BlockSpec(memory_space=pltpu.SMEM)
    out = jax.ShapeDtypeStruct((1, share, b), BF16)
    sems = 2 * CHUNKS + 2 * (n - 1) + (n - 1) + 2 * n + (n - 1) + (nz - 1) + (nx - 1) + 1
    scratch = [
        pltpu.VMEM((b, b), BF16),
        pltpu.VMEM((wl, b, b), BF16),
        pltpu.VMEM((wl, b, b), BF16),
        pltpu.VMEM((b, wl * b), BF16),
        pltpu.VMEM((wl * b, b), BF16),
        pltpu.VMEM((share, b), F32),
        pltpu.VMEM((2, n, share, b), BF16),
        pltpu.VMEM((2, n, share, b), BF16),
        pltpu.VMEM((5, 8, 128), F32),
        pltpu.VMEM((n - 1, 8, 128), F32),
        pltpu.VMEM((max(nz - 1, 1), 8, 128), F32),
        pltpu.VMEM((max(nx - 1, 1), 8, 128), F32),
        pltpu.VMEM((8, 128), F32),
        pltpu.VMEM((share, b), BF16),
        pltpu.SemaphoreType.DMA((1 + 2 * wl,)),
        pltpu.SemaphoreType.DMA((sems,)),
        pltpu.SemaphoreType.DMA((sems,)),
    ]
    scratch += [pltpu.VMEM((3, crow, b), BF16)] * CHUNKS
    scratch += [pltpu.VMEM((3, 2, share, b), BF16)] * (n // 2)
    return tuple(pl.pallas_call(
        functools.partial(kernel, dims),
        out_shape=(out, out),
        in_specs=[any_spec] * 3 + [smem] * 4,
        out_specs=(any_spec, any_spec),
        scratch_shapes=scratch,
        compiler_params=pltpu.CompilerParams(collective_id=0, has_side_effects=True),
        name="two_products",
    )(wavefunction, env_left, env_right, row_len, col_len, charge_shift, present))


def solution(mesh):
    n, ns = mesh.shape["mpo"], mesh.shape["sector"]
    nx, nz = (4, 8) if ns == 64 else (1, ns // 2)

    def body(wavefunction, env_left, env_right, row_len, col_len, charge_shift, present):
        dims = (n, ns, nx, nz, env_left.shape[0], wavefunction.shape[1])
        return shards(dims, wavefunction, env_left, env_right, row_len, col_len, charge_shift, present)

    in_specs = (
        P("sector", None, None),
        P("mpo", "sector", None, None),
        P("mpo", "sector", None, None),
        P("sector"),
        P("sector"),
        P("mpo"),
        P("mpo", "sector"),
    )
    out_specs = (P("sector", "mpo", None), P("sector", "mpo", None))
    return jax.shard_map(body, mesh=mesh, in_specs=in_specs, out_specs=out_specs, check_vma=False)
```

time: 347 us -> 76.3 us (0.22)
  waiting for transfers between devices: 185 us -> 0 us
  blocking collectives: 105 us -> 0 us
  Pallas kernels: 0 us -> 69.3 us
  starting transfers between devices: 17 us -> 0 us
  between operations: 16.2 us -> 1.93 us
  matrix products: 11.1 us -> 0 us
  other arithmetic: 9.43 us -> 0 us
    psum x2 -> x0, waiting for transfers between devices: 168 us -> none  [full_image(): return lax.psum(partial_sum, 'mpo') * cell_mask]
    psum x1 -> x0, blocking collectives: 105 us -> none  [shards(): norm_sum = lax.psum(jnp.sum(first_full * first_full), 'sector')]
    pallas_call x0 -> x1, Pallas kernels: none -> 69.3 us  [shards(): pl.pallas_call(functools.partial(kernel, dims), out_shape=(out, out), in_...]
    ppermute x4 -> x0, waiting for transfers between devices: 17.4 us -> none  [the longest x2 11.9 us: with_halo(): lax.ppermute(tail, axis, [(i, (i + 1) % count) for i in range(ends)])]
    ppermute x4 -> x0, starting transfers between devices: 16.9 us -> none  [the longest x2 12.6 us: with_halo(): lax.ppermute(head, axis, [((i + 1) % count, i) for i in range(ends)])]
    dot_general x2 -> x0, matrix products: 11.1 us -> none  [image_rows(): jnp.einsum('wij,wkj->ik', inner_part, right_envs, preferred_element_type=...]
  transfers between devices with their start and end apart: 6 -> 0, of which waited for: 6 -> 0; matrix products, arithmetic and copies ran while one was open for 1% -> 0% of each run, Pallas kernels for 0% -> 0%
where the time goes in v1:
time: 76.3 us; the launch traced here: 75.5 us
  Pallas kernels  69.3 us (91%)
  local copies, waits for them, and re-layouts  4.26 us (6%)
  between operations  1.93 us (3%)
    pallas_call x1, Pallas kernels, shards(): pl.pallas_call(functools.partial(kernel, dims), out_shape=(out, out), in_...  69.3 us
    unnamed x3, local copies, waits for them, and re-layouts  4.26 us

profile of v1, /device:TPU:6, one launch (start us, length us, event | category | flops | bytes accessed | tf_op | source)
XLA Modules:
  0.0 75.5 jit_solution(1435615354570353200)
XLA Ops:
  1.9 1.3 %copy.9.present = s32[4,1]{1,0:T(4,128)} copy(s32[4,1]{0,1:T(1,128)} %param.13) | data formatting | bytes 32 | tf_op args[6]
  3.2 69.3 %two_products.1 = (bf16[1,64,512]{2,1,0:T(8,128)(2,1)}, bf16[1,64,512]{2,1,0:T(8,128)(2,1)}) custom-call(bf16[1,512,512]{2,1,0:T(8,128)(2,1)} %wave.1, bf16[4,1,512,512]{3,2,1,0:T(8,128)(2,1)} %env_left.1, bf16[4,1,512,512]{3,2,1,0:T(8,128)(2,1)} %env_right.1, s32[1]{0:T(128)S(6)} %copy.12.row_len, s32[1]{0:T(128)S(6)} %copy.13.col_len, s32[4]{0:T(128)} %shift.1, ...), custom_call_target="tpu_custom_call" | custom-call | tf_op jit(solution)/shard_map/two_products/pallas_call | solution.py:253
  72.6 1.5 %copy.14 = bf16[1,64,512]{2,1,0:T(8,128)(2,1)} copy(bf16[1,64,512]{2,1,0:T(8,128)(2,1)} %get-tuple-element.4) | data formatting | bytes 131072
  74.1 1.5 %copy.15 = bf16[1,64,512]{2,1,0:T(8,128)(2,1)} copy(bf16[1,64,512]{2,1,0:T(8,128)(2,1)} %get-tuple-element.5) | data formatting | bytes 131072

commit v2 on v1

--- a/solution.py
+++ b/solution.py
@@ -13,8 +13,8 @@
 CHUNKS = 4
 
 
-def kernel(dims, wave, env_left, env_right, row_len, col_len, shift, present, out1, out2,
-           raw, rmat, rtrans, lcat, u, own, rs_send, rs_recv, sq_send, sq_y, sq_z, sq_x, sq_c, obuf,
+def kernel(dims, wave, env_left, env_right, row_h, col_h, shift_h, pres_h, outs, row_len, col_len, shift, present,
+           raw, rmat, rtrans, lcat, u, own, rs_send, rs_recv, sq_send, sq_y, sq_z, sq_x, sq_c, held,
            ld, ss, rs, *fields):
     n, ns, nx, nz, wl, b = dims
     h = n // 2
@@ -46,6 +46,11 @@
     for p in partners:
         pl.semaphore_signal(bar, inc=1, device_id=p, device_id_type=MESH)
 
+    small = []
+    for i, (a, t) in enumerate(((row_h, row_len), (col_h, col_len), (shift_h, shift), (pres_h, present))):
+        c = pltpu.make_async_copy(a, t, ld.at[1 + 2 * wl + i])
+        c.start()
+        small.append(c)
     load_wave = pltpu.make_async_copy(wave.at[0], raw, ld.at[0])
     load_wave.start()
     load_r, load_l = [], []
@@ -58,6 +63,8 @@
         c.start()
         load_l.append(c)
 
+    for c in small:
+        c.wait()
     rl, cl = row_len[0], col_len[0]
     near_shift = 2 * core - 1
     slot, weight = [], []
@@ -66,7 +73,7 @@
         source = s - sh
         slot.append(jnp.where(sh == 0, 0, jnp.where(sh == near_shift, 1, 2)))
         ok = jnp.logical_and(source >= 0, source < ns)
-        weight.append(jnp.where(ok, present[w, 0], 0).astype(F32))
+        weight.append(jnp.where(ok, present[0, w], 0).astype(F32))
 
     sends = []
     counter = [0]
@@ -94,9 +101,10 @@
     for c in range(CHUNKS):
         keep = jnp.logical_and(cmask, rio + c * crow < rl)
         v1[c][0] = jnp.where(keep, raw[c * crow:(c + 1) * crow, :].astype(F32), 0.0).astype(BF16)
-    pl.semaphore_wait(bar, len(partners))
+        if c == 0:
+            pl.semaphore_wait(bar, len(partners))
+        send(v1[c].at[0], v1[c].at[2], ("h1f", c), far)
     for c in range(CHUNKS):
-        send(v1[c].at[0], v1[c].at[2], ("h1f", c), far)
         send(v1[c].at[0], v1[c].at[1], ("h1n", c), near)
 
     for w in range(wl):
@@ -115,27 +123,60 @@
     def start(k):
         return pl.multiple_of(lax.rem(y + n + k, n) * share, share)
 
-    order = [h]
-    for k in range(h - 1, 0, -1):
-        order += [k, -k]
-    order += [0]
+    half = share // 2
+    low, high = pl.ds(0, half), pl.ds(half, half)
+    span = {"low": low, "high": high, "all": pl.ds(0, share)}
 
     def reduce_scatter(app, between):
-        for a in range(0, n, 2):
-            k0, k1 = order[a], order[a + 1]
+        def two_blocks(k0, k1):
             lhs = jnp.concatenate([lcat[pl.ds(start(k0), share), :], lcat[pl.ds(start(k1), share), :]], axis=0)
             part = jnp.dot(lhs, u[...], preferred_element_type=F32)
-            for k, block in ((k0, part[:share]), (k1, part[share:])):
-                if k == 0:
-                    own[...] = block
-                else:
-                    rs_send[app, k % n] = block.astype(BF16)
-                    send(rs_send.at[app, k % n], rs_recv.at[app, k % n], ("rs", app, k), ypeer(k))
+            return part[:share], part[share:]
+
+        def put(k, part, value):
+            rs_send[app, k % n, span[part]] = value.astype(BF16)
+
+        def go(k, part, hop):
+            src, dst = rs_send.at[app, k % n, span[part]], rs_recv.at[app, k % n, span[part]]
+            send(src, dst, ("rs", app, k, part), ypeer(hop))
+
+        def got(k, part):
+            arrived(rs_recv.at[app, k % n, span[part]], ("rs", app, k, part))
+            return rs_recv[app, k % n, span[part]].astype(F32)
+
+        p4, p3 = two_blocks(4, 3)
+        put(3, "all", p3)
+        put(4, "all", p4)
+        go(3, "high", 1)
+        go(4, "high", -2)
+        go(3, "low", 1)
+        go(4, "low", 2)
+        m3, p1 = two_blocks(-3, 1)
+        put(-3, "all", m3)
+        go(-3, "low", -1)
+        go(-3, "high", -1)
+        put(1, "all", p1)
+        go(1, "all", 1)
+        m1, p2 = two_blocks(-1, 2)
+        put(-1, "all", m1)
+        go(-1, "all", -1)
+        held[0] = p2
+        m2, p0 = two_blocks(-2, 0)
+        held[1] = m2
+        own[...] = p0
+        put(2, "high", held[0, high] + got(3, "high"))
+        go(2, "high", 2)
+        put(-2, "low", held[1, low] + got(-3, "low"))
+        go(-2, "low", -2)
+        put(2, "low", held[0, low] + got(3, "low") + got(4, "low"))
+        go(2, "low", 2)
+        put(-2, "high", held[1, high] + got(-3, "high") + got(4, "high"))
+        go(-2, "high", -2)
         between()
-        total = own[...]
-        for k in order[:-1]:
-            arrived(rs_recv.at[app, k % n], ("rs", app, k))
-            total = total + rs_recv[app, k % n].astype(F32)
+        total = own[...] + got(1, "all") + got(-1, "all")
+        upper = jnp.concatenate([got(-2, "low"), got(2, "high")], axis=0)
+        lower = jnp.concatenate([got(2, "low"), got(-2, "high")], axis=0)
+        total = total + upper + lower
         keep_r = lax.broadcasted_iota(jnp.int32, (share, b), 0) + y * share < rl
         keep_c = lax.broadcasted_iota(jnp.int32, (share, b), 1) < cl
         return jnp.where(jnp.logical_and(keep_r, keep_c), total, 0.0)
@@ -155,24 +196,53 @@
         tile = tile + square[:, q:q + 128]
     sq_send[0] = tile
 
+    def write_first():
+        outs[0] = v2[0][0, 0]
+
     def hand_on(r):
         send(field(r, 0), field(r, 2), ("h2f", r), far)
         send(field(r, 0), field(r, 1), ("h2n", r), near)
 
-    near_first = []
-    for k in range(1, h):
-        near_first += [k, -k]
-    near_first += [h]
-    for k in near_first:
-        send(field(0, 0), field(h if k == h else -k, 0), ("ag", h if k == h else -k), ypeer(k))
+    def pass_rows(r_here, layer_here, r_there, part, hop):
+        src, dst = field(r_here, layer_here).at[span[part]], field(r_there, 0).at[span[part]]
+        send(src, dst, ("ag", r_there, part), ypeer(hop))
+
+    def rows_in(r, part):
+        arrived(field(r, 0).at[span[part]], ("ag", r, part))
+
+    pass_rows(0, 0, -2, "low", 2)
+    pass_rows(0, 0, 2, "high", -2)
+    pass_rows(0, 0, -2, "high", 2)
+    pass_rows(0, 0, 2, "low", -2)
+    pass_rows(0, 0, -1, "all", 1)
+    pass_rows(0, 0, 1, "all", -1)
     hand_on(0)
     for k in range(1, n):
         send(sq_send.at[0], sq_y.at[k - 1], ("sqy", k), ypeer(k))
-    write1 = pltpu.make_async_copy(v2[0].at[0, 0], out1.at[0], ld.at[0])
-    write1.start()
-
-    for r in near_first:
-        arrived(field(r, 0), ("ag", r))
+    write_first()
+
+    rows_in(-2, "low")
+    pass_rows(-2, 0, 4, "low", 2)
+    pass_rows(-2, 0, -3, "low", 1)
+    rows_in(2, "high")
+    pass_rows(2, 0, 4, "high", -2)
+    pass_rows(2, 0, 3, "high", -1)
+    rows_in(-2, "high")
+    pass_rows(-2, 0, -3, "high", 1)
+    rows_in(2, "low")
+    pass_rows(2, 0, 3, "low", -1)
+    hand_on(-2)
+    hand_on(2)
+    rows_in(-1, "all")
+    hand_on(-1)
+    rows_in(1, "all")
+    hand_on(1)
+    rows_in(4, "low")
+    rows_in(4, "high")
+    hand_on(4)
+    for r in (-3, 3):
+        rows_in(r, "low")
+        rows_in(r, "high")
         hand_on(r)
 
     total = sq_send[0]
@@ -183,7 +253,7 @@
     for k in range(1, nz):
         send(sq_send.at[1], sq_z.at[k - 1], ("sqz", k), zpeer(k))
 
-    for g in list(range(1, h)) + [0]:
+    for g in (2, 1, 0, 3):
         members = (g, -g) if g else (0, h)
         for r in members:
             arrived(field(r, 1), ("h2n", r))
@@ -212,13 +282,9 @@
 
     second = reduce_scatter(1, norm_steps)
     norm = jnp.sum(sq_send[4]) / (ns * b * b) + epsilon
-    obuf[...] = (second * (1.0 / jnp.sqrt(jnp.full((1, 1), norm, F32)))).astype(BF16)
-    write2 = pltpu.make_async_copy(obuf, out2.at[0], ld.at[1])
-    write2.start()
+    outs[1] = (second * (1.0 / jnp.sqrt(jnp.full((1, 1), norm, F32)))).astype(BF16)
     for c in sends:
         c.wait_send()
-    write1.wait()
-    write2.wait()
     assert counter[0] <= ss.shape[0]
 
 
@@ -228,8 +294,9 @@
     any_spec = pl.BlockSpec(memory_space=pl.ANY)
     smem = pl.BlockSpec(memory_space=pltpu.SMEM)
     out = jax.ShapeDtypeStruct((1, share, b), BF16)
-    sems = 2 * CHUNKS + 2 * (n - 1) + (n - 1) + 2 * n + (n - 1) + (nz - 1) + (nx - 1) + 1
+    sems = 2 * CHUNKS + 24 + 12 + 2 * n + (n - 1) + (nz - 1) + (nx - 1) + 1
     scratch = [
+        pltpu.SMEM((1,), jnp.int32), pltpu.SMEM((1,), jnp.int32), pltpu.SMEM((wl,), jnp.int32), pltpu.SMEM((1, wl), jnp.int32),
         pltpu.VMEM((b, b), BF16),
         pltpu.VMEM((wl, b, b), BF16),
         pltpu.VMEM((wl, b, b), BF16),
@@ -243,22 +310,23 @@
         pltpu.VMEM((max(nz - 1, 1), 8, 128), F32),
         pltpu.VMEM((max(nx - 1, 1), 8, 128), F32),
         pltpu.VMEM((8, 128), F32),
-        pltpu.VMEM((share, b), BF16),
-        pltpu.SemaphoreType.DMA((1 + 2 * wl,)),
+        pltpu.VMEM((2, share, b), F32),
+        pltpu.SemaphoreType.DMA((5 + 2 * wl,)),
         pltpu.SemaphoreType.DMA((sems,)),
         pltpu.SemaphoreType.DMA((sems,)),
     ]
     scratch += [pltpu.VMEM((3, crow, b), BF16)] * CHUNKS
     scratch += [pltpu.VMEM((3, 2, share, b), BF16)] * (n // 2)
-    return tuple(pl.pallas_call(
+    o = pl.pallas_call(
         functools.partial(kernel, dims),
-        out_shape=(out, out),
-        in_specs=[any_spec] * 3 + [smem] * 4,
-        out_specs=(any_spec, any_spec),
+        out_shape=jax.ShapeDtypeStruct((2, share, b), BF16),
+        in_specs=[any_spec] * 7,
+        out_specs=pl.BlockSpec(memory_space=pltpu.VMEM),
         scratch_shapes=scratch,
         compiler_params=pltpu.CompilerParams(collective_id=0, has_side_effects=True),
         name="two_products",
-    )(wavefunction, env_left, env_right, row_len, col_len, charge_shift, present))
+    )(wavefunction, env_left, env_right, row_len, col_len, charge_shift, present.T)
+    return o[0:1], o[1:2]
 
 
 def solution(mesh):

time: 76.3 us -> 64.1 us (0.84)
  the two profiles are of different devices: /device:TPU:6 before, /device:TPU:1 now
where the time goes in v2:
time: 64.1 us; the launch traced here: 63.9 us
  Pallas kernels  60.5 us (94%)
  between operations  1.93 us (3%)
  local copies, waits for them, and re-layouts  1.53 us (2%)
    pallas_call x1, Pallas kernels, shards(): pl.pallas_call(functools.partial(kernel, dims), out_shape=jax.ShapeDtypeS...  60.5 us
    slice x1, local copies, waits for them, and re-layouts, shards(): return (o[0:1], o[1:2])  1.53 us

profile of v2, /device:TPU:1, one launch (start us, length us, event | category | flops | bytes accessed | tf_op | source)
XLA Modules:
  0.0 63.9 jit_solution(775701597463872730)
XLA Ops:
  1.9 60.5 %two_products.1 = bf16[2,64,512]{2,1,0:T(8,128)(2,1)} custom-call(bf16[1,512,512]{2,1,0:T(8,128)(2,1)} %wave.1, bf16[4,1,512,512]{3,2,1,0:T(8,128)(2,1)} %env_left.1, bf16[4,1,512,512]{3,2,1,0:T(8,128)(2,1)} %env_right.1, s32[1]{0:T(128)S(6)} %copy.9.row_h, s32[1]{0:T(128)S(6)} %copy.10.col_h, s32[4]{0:T(128)} %shift_h.1, s32[1,4]{1,0:T(1,128)} %bitcast.1), custom_call_target="tpu_custom_call" | custom-call | tf_op jit(solution)/shard_map/two_products/pallas_call | solution.py:320
  62.4 1.5 %fusion = (bf16[1,64,512]{2,1,0:T(8,128)(2,1)}, bf16[1,64,512]{2,1,0:T(8,128)(2,1)}) fusion(bf16[2,64,512]{2,1,0:T(8,128)(2,1)} %two_products.1), kind=kLoop, calls=%fused_computation | loop fusion | bytes 262144 | tf_op jit(solution)/shard_map/slice | solution.py:329

commit v3 on v2

--- a/solution.py
+++ b/solution.py
@@ -127,7 +127,7 @@
     low, high = pl.ds(0, half), pl.ds(half, half)
     span = {"low": low, "high": high, "all": pl.ds(0, share)}
 
-    def reduce_scatter(app, between):
+    def reduce_scatter(app, midway=None, between=None):
         def two_blocks(k0, k1):
             lhs = jnp.concatenate([lcat[pl.ds(start(k0), share), :], lcat[pl.ds(start(k1), share), :]], axis=0)
             part = jnp.dot(lhs, u[...], preferred_element_type=F32)
@@ -168,11 +168,14 @@
         go(2, "high", 2)
         put(-2, "low", held[1, low] + got(-3, "low"))
         go(-2, "low", -2)
+        if midway is not None:
+            midway()
         put(2, "low", held[0, low] + got(3, "low") + got(4, "low"))
         go(2, "low", 2)
         put(-2, "high", held[1, high] + got(-3, "high") + got(4, "high"))
         go(-2, "high", -2)
-        between()
+        if between is not None:
+            between()
         total = own[...] + got(1, "all") + got(-1, "all")
         upper = jnp.concatenate([got(-2, "low"), got(2, "high")], axis=0)
         lower = jnp.concatenate([got(2, "low"), got(-2, "high")], axis=0)
@@ -181,7 +184,7 @@
         keep_c = lax.broadcasted_iota(jnp.int32, (share, b), 1) < cl
         return jnp.where(jnp.logical_and(keep_r, keep_c), total, 0.0)
 
-    image = reduce_scatter(0, lambda: None)
+    image = reduce_scatter(0)
 
     def field(r, layer):
         if r in (0, h):
@@ -264,25 +267,28 @@
             for i, r in enumerate(members):
                 u[pl.ds(w * b + start(r), share), :] = part[i * share:(i + 1) * share]
 
-    def norm_steps():
-        total = sq_send[1]
-        for k in range(1, nz):
-            arrived(sq_z.at[k - 1], ("sqz", k))
-            total = total + sq_z[k - 1]
-        sq_send[2] = total
-        for k in range(1, nx):
-            send(sq_send.at[2], sq_x.at[k - 1], ("sqx", k), xpeer(k))
+    for k in range(1, nz):
+        arrived(sq_z.at[k - 1], ("sqz", k))
+        total = total + sq_z[k - 1]
+    sq_send[2] = total
+    for k in range(1, nx):
+        send(sq_send.at[2], sq_x.at[k - 1], ("sqx", k), xpeer(k))
+
+    def collect_x():
+        total = sq_send[2]
         for k in range(1, nx):
             arrived(sq_x.at[k - 1], ("sqx", k))
             total = total + sq_x[k - 1]
         sq_send[3] = total
         send(sq_send.at[3], sq_c, ("sqc", 0), near)
+
+    def collect_core():
         arrived(sq_c, ("sqc", 0))
-        sq_send[4] = total + sq_c[...]
-
-    second = reduce_scatter(1, norm_steps)
-    norm = jnp.sum(sq_send[4]) / (ns * b * b) + epsilon
-    outs[1] = (second * (1.0 / jnp.sqrt(jnp.full((1, 1), norm, F32)))).astype(BF16)
+        norm = jnp.sum(sq_send[3] + sq_c[...]) / (ns * b * b) + epsilon
+        sq_send[4] = 1.0 / jnp.sqrt(jnp.full((8, 128), norm, F32))
+
+    second = reduce_scatter(1, collect_x, collect_core)
+    outs[1] = (second * sq_send[4, 0:1, 0:1]).astype(BF16)
     for c in sends:
         c.wait_send()
     assert counter[0] <= ss.shape[0]

time: 64.1 us -> 62.8 us (0.980)
  the two profiles are of different devices: /device:TPU:1 before, /device:TPU:6 now
where the time goes in v3:
time: 62.8 us; the launch traced here: 62 us
  Pallas kernels  58.5 us (93%)
  between operations  1.93 us (3%)
  local copies, waits for them, and re-layouts  1.53 us (2%)
    pallas_call x1, Pallas kernels, shards(): pl.pallas_call(functools.partial(kernel, dims), out_shape=jax.ShapeDtypeS...  58.5 us
    slice x1, local copies, waits for them, and re-layouts, shards(): return (o[0:1], o[1:2])  1.53 us

profile of v3, /device:TPU:6, one launch (start us, length us, event | category | flops | bytes accessed | tf_op | source)
XLA Modules:
  0.0 62.0 jit_solution(7673389612573885901)
XLA Ops:
  1.9 58.5 %two_products.1 = bf16[2,64,512]{2,1,0:T(8,128)(2,1)} custom-call(bf16[1,512,512]{2,1,0:T(8,128)(2,1)} %wave.1, bf16[4,1,512,512]{3,2,1,0:T(8,128)(2,1)} %env_left.1, bf16[4,1,512,512]{3,2,1,0:T(8,128)(2,1)} %env_right.1, s32[1]{0:T(128)S(6)} %copy.9.row_h, s32[1]{0:T(128)S(6)} %copy.10.col_h, s32[4]{0:T(128)} %shift_h.1, s32[1,4]{1,0:T(1,128)} %bitcast.1), custom_call_target="tpu_custom_call" | custom-call | tf_op jit(solution)/shard_map/two_products/pallas_call | solution.py:326
  60.4 1.5 %fusion = (bf16[1,64,512]{2,1,0:T(8,128)(2,1)}, bf16[1,64,512]{2,1,0:T(8,128)(2,1)}) fusion(bf16[2,64,512]{2,1,0:T(8,128)(2,1)} %two_products.1), kind=kLoop, calls=%fused_computation | loop fusion | bytes 262144 | tf_op jit(solution)/shard_map/slice | solution.py:335

commit v4 on v3

--- a/solution.py
+++ b/solution.py
@@ -85,15 +85,29 @@
             counter[0] += 1
         return sem_of[key]
 
+    has_far = jnp.logical_and(s + 2 * core > 0, s + 2 * core < ns + 1)
+
     def send(src, dst, key, dev):
         i = sem(key)
         c = pltpu.make_async_remote_copy(src, dst, ss.at[i], rs.at[i], device_id=dev, device_id_type=MESH)
-        c.start()
-        sends.append(c)
-
-    def arrived(dst, key):
+        if dev is far:
+            pl.when(has_far)(c.start)
+        else:
+            c.start()
+        sends.append((c, dev is far))
+
+    def arrived(dst, key, from_far=False):
         i = sem(key)
-        pltpu.make_async_remote_copy(dst, dst, ss.at[i], rs.at[i], device_id=near, device_id_type=MESH).wait_recv()
+        c = pltpu.make_async_remote_copy(dst, dst, ss.at[i], rs.at[i], device_id=near, device_id_type=MESH)
+        if from_far:
+            pl.when(has_far)(c.wait_recv)
+        else:
+            c.wait_recv()
+
+    @pl.when(jnp.logical_not(has_far))
+    def _():
+        for f in fields:
+            f[2] = jnp.zeros(f.shape[1:], BF16)
 
     load_wave.wait()
     cmask = lax.broadcasted_iota(jnp.int32, (crow, b), 1) < cl
@@ -115,7 +129,7 @@
 
     for c in range(CHUNKS):
         arrived(v1[c].at[1], ("h1n", c))
-        arrived(v1[c].at[2], ("h1f", c))
+        arrived(v1[c].at[2], ("h1f", c), True)
         for w in range(wl):
             part = jnp.dot(v1[c][slot[w]], rtrans[w], preferred_element_type=F32)
             u[w * b + c * crow:w * b + (c + 1) * crow, :] = (part * weight[w]).astype(BF16)
@@ -260,7 +274,7 @@
         members = (g, -g) if g else (0, h)
         for r in members:
             arrived(field(r, 1), ("h2n", r))
-            arrived(field(r, 2), ("h2f", r))
+            arrived(field(r, 2), ("h2f", r), True)
         for w in range(wl):
             lhs = v2[g][slot[w]].reshape(2 * share, b)
             part = (jnp.dot(lhs, rtrans[w], preferred_element_type=F32) * weight[w]).astype(BF16)
@@ -289,8 +303,11 @@
 
     second = reduce_scatter(1, collect_x, collect_core)
     outs[1] = (second * sq_send[4, 0:1, 0:1]).astype(BF16)
-    for c in sends:
-        c.wait_send()
+    for c, to_far in sends:
+        if to_far:
+            pl.when(has_far)(c.wait_send)
+        else:
+            c.wait_send()
     assert counter[0] <= ss.shape[0]
 
 

time: 62.8 us -> 62.7 us (level)
  no operation moved by 1% of the time
where the time goes in v4:
time: 62.7 us; the launch traced here: 62 us
  Pallas kernels  58.5 us (93%)
  between operations  1.93 us (3%)
  local copies, waits for them, and re-layouts  1.53 us (2%)
    pallas_call x1, Pallas kernels, shards(): pl.pallas_call(functools.partial(kernel, dims), out_shape=jax.ShapeDtypeS...  58.5 us
    slice x1, local copies, waits for them, and re-layouts, shards(): return (o[0:1], o[1:2])  1.53 us

profile of v4, /device:TPU:6, one launch (start us, length us, event | category | flops | bytes accessed | tf_op | source)
XLA Modules:
  0.0 62.0 jit_solution(17156888902984261893)
XLA Ops:
  1.9 58.5 %two_products.1 = bf16[2,64,512]{2,1,0:T(8,128)(2,1)} custom-call(bf16[1,512,512]{2,1,0:T(8,128)(2,1)} %wave.1, bf16[4,1,512,512]{3,2,1,0:T(8,128)(2,1)} %env_left.1, bf16[4,1,512,512]{3,2,1,0:T(8,128)(2,1)} %env_right.1, s32[1]{0:T(128)S(6)} %copy.9.row_h, s32[1]{0:T(128)S(6)} %copy.10.col_h, s32[4]{0:T(128)} %shift_h.1, s32[1,4]{1,0:T(1,128)} %bitcast.1), custom_call_target="tpu_custom_call" | custom-call | tf_op jit(solution)/shard_map/two_products/pallas_call | solution.py:343
  60.4 1.5 %fusion = (bf16[1,64,512]{2,1,0:T(8,128)(2,1)}, bf16[1,64,512]{2,1,0:T(8,128)(2,1)}) fusion(bf16[2,64,512]{2,1,0:T(8,128)(2,1)} %two_products.1), kind=kLoop, calls=%fused_computation | loop fusion | bytes 262144 | tf_op jit(solution)/shard_map/slice | solution.py:352
